TPU v7x, 256 devices: a whole 4x4x8 slice. The times are simulated.
256 devices in a mesh: tp: 16 (over x, z_lo), hb: 16 (over y, z_hi, core).
Axes of the slice: x: 4, y: 4, z: 8 (z_hi: 2, z_lo: 4; z = z_hi * 4 + z_lo), core: 2. Of those that a mesh axis runs over, the one named last changes fastest.
Arguments:
- normed: bfloat16 [2048, 16384], P('hb', 'tp'), may hold values from -6 to 6
- hidden: bfloat16 [2048, 26624], P('hb', 'tp'), may hold values from -6 to 6
Outputs:
- h_in: float32 [16384, 16384], P('tp', 'hb')
- h_down: float32 [26624, 1664], P(('tp', 'hb'))
All inputs are finite; a program needn't handle non-finite values.
Results may differ from a plain program's by a relative error of at most 0.0003.
Values may be sent and summed in bfloat16 or wider, within the bound.
No kernel may reach another device: no remote copies, remote signals or barrier semaphores. Data moves between devices by JAX's collectives and lax.ppermute only.
A program may use at most 128 MiB of HBM per device.

v0:
```python
import jax
import jax.numpy as jnp
from jax import lax
from jax.sharding import PartitionSpec as P


def gram_product(left, right):
    return lax.dot_general(
        left, right, (((0,), (0,)), ((), ())), preferred_element_type=jnp.float32
    )


def per_device(normed, hidden):
    groups = lax.axis_size("hb")
    scale = 2.0 / (normed.shape[0] * groups)
    whole_rows = lax.all_gather(normed, "tp", axis=1, tiled=True)
    columns = lax.all_to_all(whole_rows, "hb", split_axis=1, concat_axis=0, tiled=True)
    part = columns
    h_in = gram_product(lax.all_gather(normed, "hb", axis=0, tiled=True), part) * scale
    part = hidden
    h_down = (
        lax.psum_scatter(gram_product(part, hidden), "hb", scatter_dimension=0, tiled=True) * scale
    )
    return (h_in, h_down)


def solution(mesh):
    return jax.shard_map(
        per_device,
        mesh=mesh,
        in_specs=(P("hb", "tp"), P("hb", "tp")),
        out_specs=(P("tp", "hb"), P(("tp", "hb"), None)),
        check_vma=False,
    )
```

profile of v0, /device:TPU:2, one launch (start us, length us, event | category | flops | bytes accessed | tf_op | source)
XLA Modules:
  0.0 419.3 jit_solution(16098393865919439729)
XLA Ops:
  7.2 0.0 copy-start
  7.2 0.0 all-gather.5.cloned.1.call-start
  7.2 1.8 copy.6
  9.1 0.0 all-gather.5.cloned.1.call-update
  9.1 0.0 all-gather.3.cloned.1.call-start
  9.1 0.7 all-gather.3.cloned.1.call-update
  9.8 0.0 reduce-scatter.4.cloned.1.call-start
  9.9 0.0 copy-done
  9.9 5.8 %fusion = f32[1664,1664]{1,0:T(8,128)} fusion(bf16[128,1664]{1,0:T(8,128)(2,1)S(1)} %copy-done), kind=kOutput, calls=%fused_computation.2 | convolution fusion | flops 708837376 | bytes 11501568 | tf_op jit(solution)/shard_map/dot_general | solution.py:8
  15.7 0.0 reduce-scatter.4.cloned.1.call-update
  15.8 97.4 %all-gather.5.cloned.1.call-done = bf16[128,16384]{0,1:T(8,128)(2,1)} async-done(((bf16[128,1024]{0,1:T(8,128)(2,1)}), bf16[128,16384]{0,1:T(8,128)(2,1)}) %all-gather.5.cloned.1.call-update) | async-done | bytes 4194320 | tf_op jit(solution)/shard_map/all_gather | solution.py:16
  113.2 134.0 %all_to_all.19 = bf16[128,16,1024]{0,2,1:T(8,128)(2,1)} all-to-all(bf16[128,16,1024]{0,2,1:T(8,128)(2,1)} %bitcast.9), channel_id=1, replica_groups=mesh['tp'=16,'hb'=16] {'hb'}, dimensions={1} | all-to-all | bytes 8388608 | tf_op jit(solution)/shard_map/all_to_all | solution.py:17
  247.1 6.4 %copy.7 = bf16[16,128,1024]{2,1,0:T(8,128)(2,1)} copy(bf16[16,128,1024]{1,2,0:T(8,128)(2,1)} %bitcast.8) | data formatting | bytes 8388608 | tf_op jit(solution)/shard_map/all_to_all | solution.py:17
  253.6 0.0 all-gather.3.cloned.1.call-done
  253.6 10.9 %convolution_multiply_fusion = f32[1024,1024]{1,0:T(8,128)} fusion(bf16[2048,1024]{1,0:T(8,128)(2,1)} %all-gather.3.cloned.1.call-done, bf16[2048,1024]{1,0:T(8,128)(2,1)} %bitcast.10), kind=kOutput, calls=%fused_computation | convolution fusion | flops 4296015872 | bytes 12582912 | tf_op jit(solution)/shard_map/dot_general | solution.py:8
  264.5 146.2 %reduce-scatter.4.cloned.1.call-done = f32[104,1664]{1,0:T(8,128)} async-done(((f32[1664,1664]{1,0:T(8,128)}), f32[104,1664]{1,0:T(8,128)}) %reduce-scatter.4.cloned.1.call-update) | async-done | bytes 692240
  410.8 2.0 broadcast_multiply_fusion
Async XLA Ops:
  7.2 2.7 copy-start
  7.2 106.0 %all-gather.5.cloned.1.call-start = ((), (), s32[]{:S(2)}) async-start(), calls=%async_computation.3 | async-start | bytes 4456448 | tf_op jit(solution)/shard_map/all_gather | solution.py:16
  9.1 244.5 %all-gather.3.cloned.1.call-start = ((), (), s32[]{:S(2)}) async-start(), calls=%async_computation.2 | async-start | bytes 4456448 | tf_op jit(solution)/shard_map/all_gather | solution.py:19
  9.8 400.9 %reduce-scatter.4.cloned.1.call-start = ((), (), s32[]{:S(2)}) async-start(), calls=%async_computation.4 | async-start | bytes 11767808
Sparse Core Ops, SparseCore 0:
  10.4 102.7 all-gather.4
  115.9 106.8 all-gather.2
  227.3 183.4 reduce-scatter.3
where the time goes:
time: 420 us; the launch traced here: 419 us
  waiting for transfers between devices  244 us (58%)
  blocking collectives  134 us (32%)
  matrix products  16.8 us (4%)
  between operations  13.8 us (3%)
  local copies, waits for them, and re-layouts  8.29 us (2%)
    unnamed x4, waiting for transfers between devices  147 us
    all_to_all x1, blocking collectives, per_device(): lax.all_to_all(whole_rows, 'hb', split_axis=1, concat_axis=0, tiled=True)  134 us
    all_gather x1, waiting for transfers between devices, per_device(): whole_rows = lax.all_gather(normed, 'tp', axis=1, tiled=True)  97.4 us
    dot_general x2, matrix products, gram_product(): lax.dot_general(left, right, (((0,), (0,)), ((), ())), preferred_element_...  16.8 us
  transfers between devices with their start and end apart: 3, of which 2 were waited for; matrix products, arithmetic and copies ran while one was open for 6% of the time, Pallas kernels for 0%

commit v1 on v0

--- a/solution.py
+++ b/solution.py
@@ -13,7 +13,8 @@
 def per_device(normed, hidden):
     groups = lax.axis_size("hb")
     scale = 2.0 / (normed.shape[0] * groups)
-    whole_rows = lax.all_gather(normed, "tp", axis=1, tiled=True)
+    sent = jnp.stack([normed] * lax.axis_size("tp"))
+    whole_rows = jnp.concatenate(lax.all_to_all(sent, "tp", 0, 0), axis=1)
     columns = lax.all_to_all(whole_rows, "hb", split_axis=1, concat_axis=0, tiled=True)
     part = columns
     h_in = gram_product(lax.all_gather(normed, "hb", axis=0, tiled=True), part) * scale

time: 420 us -> 363 us (0.86)
  blocking collectives: 134 us -> 0 us
  waiting for transfers between devices: 244 us -> 310 us
  starting transfers between devices: 0.12 us -> 17.5 us
  local copies, waits for them, and re-layouts: 8.29 us -> 3.51 us
    all_to_all x0 -> x2, waiting for transfers between devices: none -> 256 us  [the longest x1 140 us: per_device(): lax.all_to_all(whole_rows, 'hb', split_axis=1, concat_axis=0, tiled=True)]
    all_to_all x1 -> x0, blocking collectives: 134 us -> none  [per_device(): lax.all_to_all(whole_rows, 'hb', split_axis=1, concat_axis=0, tiled=True)]
    all_gather x1 -> x0, waiting for transfers between devices: 97.4 us -> none  [per_device(): whole_rows = lax.all_gather(normed, 'tp', axis=1, tiled=True)]
    unnamed x4 -> x3, waiting for transfers between devices: 147 us -> 53.9 us
    all_to_all x0 -> x2, starting transfers between devices: none -> 17.5 us  [the longest x1 8.91 us: per_device(): whole_rows = jnp.concatenate(lax.all_to_all(sent, 'tp', 0, 0), axis=1)]
    all_to_all x1 -> x0, local copies, waits for them, and re-layouts: 6.45 us -> none  [per_device(): lax.all_to_all(whole_rows, 'hb', split_axis=1, concat_axis=0, tiled=True)]
  transfers between devices with their start and end apart: 3 -> 4, of which waited for: 2 -> 3; matrix products, arithmetic and copies ran while one was open for 6% -> 5% of each run, Pallas kernels for 0% -> 0%
where the time goes in v1:
time: 363 us
  waiting for transfers between devices  310 us (85%)
  starting transfers between devices  17.5 us (5%)
  matrix products  16.2 us (4%)
  between operations  14.1 us (4%)
    all_to_all x1, waiting for transfers between devices, per_device(): lax.all_to_all(whole_rows, 'hb', split_axis=1, concat_axis=0, tiled=True)  140 us
    all_to_all x1, waiting for transfers between devices, per_device(): whole_rows = jnp.concatenate(lax.all_to_all(sent, 'tp', 0, 0), axis=1)  116 us
    unnamed x3, waiting for transfers between devices  53.9 us
    dot_general x2, matrix products, gram_product(): lax.dot_general(left, right, (((0,), (0,)), ((), ())), preferred_element_...  16.2 us
    all_to_all x1, starting transfers between devices, per_device(): whole_rows = jnp.concatenate(lax.all_to_all(sent, 'tp', 0, 0), axis=1)  8.91 us
    all_to_all x1, starting transfers between devices, per_device(): lax.all_to_all(whole_rows, 'hb', split_axis=1, concat_axis=0, tiled=True)  8.55 us
  transfers between devices with their start and end apart: 4, of which 3 were waited for; matrix products, arithmetic and copies ran while one was open for 5% of the time, Pallas kernels for 0%

profile of v1, /device:TPU:2, one launch (start us, length us, event | category | flops | bytes accessed | tf_op | source)
XLA Modules:
  0.0 363.2 jit_solution(1168298404028890197)
XLA Ops:
  7.2 0.0 copy-start
  7.2 0.0 all-gather.2.cloned.1.call-start
  7.2 0.7 all-gather.2.cloned.1.call-update
  7.9 3.5 stack.2
  11.4 8.9 %all-to-all-start = ((bf16[16,128,1024]{2,1,0:T(8,128)(2,1)}), bf16[16,128,1024]{2,1,0:T(8,128)(2,1)}, u32[]{:S(2)}, u32[]{:S(2)}) async-start(bf16[16,128,1024]{2,1,0:T(8,128)(2,1)} %stack.2), calls=%async_computation | async-start | bytes 8388608 | tf_op jit(solution)/shard_map/all_to_all | solution.py:17
  20.3 0.0 reduce-scatter.4.cloned.1.call-start
  20.4 0.0 copy-done
  20.4 5.8 %fusion = f32[1664,1664]{1,0:T(8,128)} fusion(bf16[128,1664]{1,0:T(8,128)(2,1)S(1)} %copy-done), kind=kOutput, calls=%fused_computation.2 | convolution fusion | flops 708837376 | bytes 11501568 | tf_op jit(solution)/shard_map/dot_general | solution.py:8
  26.2 0.0 reduce-scatter.4.cloned.1.call-update
  26.2 115.7 %all-to-all-done = bf16[16,128,1024]{2,1,0:T(8,128)(2,1)} async-done(((bf16[16,128,1024]{2,1,0:T(8,128)(2,1)}), bf16[16,128,1024]{2,1,0:T(8,128)(2,1)}, u32[]{:S(2)}, u32[]{:S(2)}) %all-to-all-start) | async-done | bytes 4194336 | tf_op jit(solution)/shard_map/all_to_all | solution.py:17
  142.0 8.6 %all-to-all-start.1 = ((bf16[128,16,1024]{2,0,1:T(8,128)(2,1)}), bf16[128,16,1024]{2,0,1:T(8,128)(2,1)}, u32[]{:S(2)}, u32[]{:S(2)}) async-start(bf16[128,16,1024]{2,0,1:T(8,128)(2,1)} %bitcast), calls=%async_computation.1 | async-start | bytes 8388608 | tf_op jit(solution)/shard_map/all_to_all | solution.py:18
  150.5 0.0 all-gather.2.cloned.1.call-done
  150.6 140.1 %all-to-all-done.1 = bf16[128,16,1024]{2,0,1:T(8,128)(2,1)} async-done(((bf16[128,16,1024]{2,0,1:T(8,128)(2,1)}), bf16[128,16,1024]{2,0,1:T(8,128)(2,1)}, u32[]{:S(2)}, u32[]{:S(2)}) %all-to-all-start.1) | async-done | bytes 4194336 | tf_op jit(solution)/shard_map/all_to_all | solution.py:18
  290.7 10.4 %convolution_multiply_fusion = f32[1024,1024]{1,0:T(8,128)} fusion(bf16[2048,1024]{1,0:T(8,128)(2,1)} %all-gather.2.cloned.1.call-done, bf16[2048,1024]{1,0:T(8,128)(2,1)} %bitcast.2), kind=kOutput, calls=%fused_computation | convolution fusion | flops 4296015872 | bytes 12582912 | tf_op jit(solution)/shard_map/dot_general | solution.py:8
  301.1 53.2 %reduce-scatter.4.cloned.1.call-done = f32[104,1664]{1,0:T(8,128)} async-done(((f32[1664,1664]{1,0:T(8,128)}), f32[104,1664]{1,0:T(8,128)}) %reduce-scatter.4.cloned.1.call-update) | async-done | bytes 692240
  354.4 2.0 broadcast_multiply_fusion
Async XLA Ops:
  7.2 13.2 %copy-start = (bf16[128,1664]{1,0:T(8,128)(2,1)S(1)}, bf16[128,1664]{1,0:T(8,128)(2,1)}, u32[]{:S(2)}) copy-start(bf16[128,1664]{1,0:T(8,128)(2,1)} %param.3) | copy-start | bytes 1277956
  7.2 143.4 %all-gather.2.cloned.1.call-start = ((), (), s32[]{:S(2)}) async-start(), calls=%async_computation.3 | async-start | bytes 4456448 | tf_op jit(solution)/shard_map/all_gather | solution.py:20
  11.4 130.6 %all-to-all-start = ((bf16[16,128,1024]{2,1,0:T(8,128)(2,1)}), bf16[16,128,1024]{2,1,0:T(8,128)(2,1)}, u32[]{:S(2)}, u32[]{:S(2)}) async-start(bf16[16,128,1024]{2,1,0:T(8,128)(2,1)} %stack.2), calls=%async_computation | async-start | bytes 8388608 | tf_op jit(solution)/shard_map/all_to_all | solution.py:17
  20.3 334.0 %reduce-scatter.4.cloned.1.call-start = ((), (), s32[]{:S(2)}) async-start(), calls=%async_computation.4 | async-start | bytes 11767808
  142.0 148.7 %all-to-all-start.1 = ((bf16[128,16,1024]{2,0,1:T(8,128)(2,1)}), bf16[128,16,1024]{2,0,1:T(8,128)(2,1)}, u32[]{:S(2)}, u32[]{:S(2)}) async-start(bf16[128,16,1024]{2,0,1:T(8,128)(2,1)} %bitcast), calls=%async_computation.1 | async-start | bytes 8388608 | tf_op jit(solution)/shard_map/all_to_all | solution.py:18
Sparse Core Ops, SparseCore 0:
  10.7 82.2 all-gather.1
  97.6 256.7 reduce-scatter.3
